TPU v7x, 32 devices: a whole 2x2x4 slice. The times are simulated.
32 devices in a mesh: dp: 4 (over y, x), expert: 4 (over z), tok: 2 (over core).
Axes of the slice: x: 2, y: 2, z: 4, core: 2. Of those that a mesh axis runs over, the one named last changes fastest.
Arguments:
- tokens: bfloat16 [32768, 512], P(('dp', 'expert', 'tok')), may hold values from -6 to 6
- out_grad: bfloat16 [32768, 512], P(('dp', 'expert', 'tok')), may hold values from -6 to 6
- expert_ids: int32 [32768, 2], P(('dp', 'expert', 'tok')), may hold values from 0 to 3, all different within a row; in each aligned block of 1024 rows (0 to 1023, 1024 to 2047, ...) at most 768 rows name the same one
- sentence_ids: int32 [32, 1024], P(('dp', 'expert', 'tok')), may hold values from 0 to 15, never falling along the last dimension, each value on 1 to 128 neighbouring positions
- ln_attn: float32 [512], replicated, may hold values from 0.25 to 1.75
- w_kv: bfloat16 [512, 128], replicated, may hold values from -0.25 to 0.25
- w_router: bfloat16 [512, 4], replicated, may hold values from -0.1875 to 0.1875
- w_query: bfloat16 [4, 512, 64], P('expert'), may hold values from -0.25 to 0.25
- w_output: bfloat16 [4, 64, 512], P('expert'), may hold values from -4 to 4
- ln_ffn: float32 [512], replicated, may hold values from 0.25 to 1.75
- w_in: bfloat16 [512, 2048], replicated, may hold values from -0.25 to 0.25
- w_out: bfloat16 [2048, 512], replicated, may hold values from -0.1875 to 0.1875
Outputs:
- output: bfloat16 [32768, 512], P(('dp', 'expert', 'tok'))
- grad_tokens: bfloat16 [32768, 512], P(('dp', 'expert', 'tok'))
- grad_ln_attn: float32 [512], replicated
- grad_kv: float32 [512, 128], replicated
- grad_router: float32 [512, 4], replicated
- grad_query: float32 [4, 512, 64], P('expert')
- grad_output: float32 [4, 64, 512], P('expert')
- grad_ln_ffn: float32 [512], replicated
- grad_in: float32 [512, 2048], replicated
- grad_out: float32 [2048, 512], replicated
Inputs may be any that keep to these rules, and one draw needn't show every extreme that they name: `expert_ids`: among the 1024 rows of one device no expert is named more than 768 times, a bound that some block reaches; a token's 2 ids differ. `sentence_ids`: in each device's row the ids never fall; each id covers 1 to 128 consecutive positions, one exactly 128.
All inputs are finite; a program needn't handle non-finite values.
Results may differ from a plain program's by a relative error of at most 0.017.
Values may be sent and summed in bfloat16 or wider, within the bound.
No kernel may reach another device: no remote copies, remote signals or barrier semaphores. Data moves between devices by JAX's collectives and lax.ppermute only.
A program may use at most 128 MiB of HBM per device.

v0:
```python
import jax
import jax.numpy as jnp
from jax import lax
from jax.sharding import PartitionSpec as P


def product(left, right):
    return jnp.dot(left, right, preferred_element_type=jnp.float32)


def product_tn(left, right):
    return lax.dot_general(
        left, right, (((0,), (0,)), ((), ())), preferred_element_type=jnp.float32
    )


def product_nt(left, right):
    return lax.dot_general(
        left, right, (((1,), (1,)), ((), ())), preferred_element_type=jnp.float32
    )


def layer_norm_parts(values, gain):
    centre = values - jnp.mean(values, axis=-1, keepdims=True)
    spread = jnp.mean(centre * centre, axis=-1, keepdims=True)
    inverse = lax.rsqrt(spread + 1e-05)
    normalized = centre * inverse
    return (normalized * gain, normalized, inverse)


def layer_norm_back(upstream, normalized, inverse, gain):
    scaled = upstream * gain
    gain_grad = jnp.sum(upstream * normalized, axis=0)
    inner = (
        scaled
        - jnp.mean(scaled, axis=-1, keepdims=True)
        - normalized * jnp.mean(scaled * normalized, axis=-1, keepdims=True)
    )
    return (inner * inverse, gain_grad)


def gelu_exact(values):
    return 0.5 * values * (1.0 + jax.scipy.special.erf(values * 0.7071067811865476))


def gelu_slope(values):
    cumulative = 0.5 * (1.0 + jax.scipy.special.erf(values * 0.7071067811865476))
    density = jnp.exp(-0.5 * values * values) * 0.3989422804014327
    return cumulative + values * density


def head_forward(rows, row_ids, shared, key_ids, query_weight, output_weight):
    head_size = query_weight.shape[1]
    queries = product(rows, query_weight).astype(jnp.bfloat16)
    scores = product_nt(queries, shared[:, :head_size]) * 0.125
    scores = jnp.where(row_ids[:, None] == key_ids[None, :], scores, -30000.0)
    largest = jnp.max(scores, axis=-1, keepdims=True)
    raised = jnp.exp(scores - largest)
    total = jnp.sum(raised, axis=-1, keepdims=True)
    weights = (raised / total).astype(jnp.bfloat16)
    attended = product(weights, shared[:, head_size:]).astype(jnp.bfloat16)
    result = product(attended, output_weight).astype(jnp.bfloat16)
    log_total = largest[:, 0] + jnp.log(total[:, 0])
    return (result, queries, attended, log_total)


def head_backward(
    rows,
    row_ids,
    shared,
    key_ids,
    query_weight,
    output_weight,
    queries,
    attended,
    log_total,
    result_grad,
):
    head_size = query_weight.shape[1]
    output_grad = product_tn(attended, result_grad)
    attended_grad = product_nt(result_grad, output_weight).astype(jnp.bfloat16)
    scores = product_nt(queries, shared[:, :head_size]) * 0.125
    scores = jnp.where(row_ids[:, None] == key_ids[None, :], scores, -30000.0)
    probs = jnp.exp(scores - log_total[:, None])
    prob_low = probs.astype(jnp.bfloat16)
    prob_grad = product_nt(attended_grad, shared[:, head_size:])
    score_grad = (probs * (prob_grad - jnp.sum(probs * prob_grad, axis=-1, keepdims=True))).astype(
        jnp.bfloat16
    )
    query_grad = (product(score_grad, shared[:, :head_size]) * 0.125).astype(jnp.bfloat16)
    key_grad = product_tn(score_grad, queries) * 0.125
    value_grad = product_tn(prob_low, attended_grad)
    shared_grad = jnp.concatenate([key_grad, value_grad], axis=1)
    query_weight_grad = product_tn(rows, query_grad)
    rows_grad = product_nt(query_grad, query_weight).astype(jnp.bfloat16)
    return (rows_grad, shared_grad, query_weight_grad, output_grad)


def body(
    tokens,
    out_grad,
    expert_ids,
    sentence_ids,
    ln_attn,
    w_kv,
    w_router,
    w_query,
    w_output,
    ln_ffn,
    w_in,
    w_out,
):
    length = tokens.shape[0]
    width = tokens.shape[1]
    choose = expert_ids.shape[1]
    head_size = w_query.shape[2]
    experts = lax.axis_size("expert")
    capacity = 3 * length // experts
    sentence = sentence_ids[0]
    inputs = tokens.astype(jnp.float32)
    normed, norm_one, inverse_one = layer_norm_parts(inputs, ln_attn)
    normed_low = normed.astype(jnp.bfloat16)
    shared = product(normed_low, w_kv).astype(jnp.bfloat16)
    logits = product(normed_low, w_router)
    expert_range = jnp.arange(experts, dtype=jnp.int32)
    selector = (expert_ids[:, :, None] == expert_range[None, None, :]).astype(jnp.float32)
    picked = jnp.sum(selector * logits[:, None, :], axis=2)
    picked_top = jnp.max(picked, axis=-1, keepdims=True)
    picked_raised = jnp.exp(picked - picked_top)
    gates = picked_raised / jnp.sum(picked_raised, axis=-1, keepdims=True)
    flat_expert = expert_ids.reshape(length * choose)
    member = (flat_expert[:, None] == expert_range[None, :]).astype(jnp.int32)
    earlier = jnp.cumsum(member, axis=0) - member
    position = jnp.sum(earlier * member, axis=1)
    slot_index = flat_expert * capacity + position
    routed_rows = jnp.broadcast_to(normed_low[:, None, :], (length, choose, width)).reshape(
        length * choose, width
    )
    routed_ids = jnp.broadcast_to(sentence[:, None], (length, choose)).reshape(length * choose)
    dispatch_rows = (
        jnp.zeros((experts * capacity, width), jnp.bfloat16)
        .at[slot_index]
        .set(routed_rows)
        .reshape(experts, capacity, width)
    )
    dispatch_ids = (
        jnp.full((experts * capacity,), -1, jnp.int32)
        .at[slot_index]
        .set(routed_ids)
        .reshape(experts, capacity)
    )
    arrived, arrived_ids = (
        lax.all_to_all(dispatch_rows, "expert", split_axis=0, concat_axis=0, tiled=True),
        lax.all_to_all(dispatch_ids, "expert", split_axis=0, concat_axis=0, tiled=True),
    )
    all_shared, all_ids = (
        lax.all_gather(shared, "expert", axis=0, tiled=True),
        lax.all_gather(sentence, "expert", axis=0, tiled=True),
    )
    all_shared = all_shared.reshape(experts, length, 2 * head_size)
    all_ids = all_ids.reshape(experts, length)
    own_query = w_query[0]
    own_output = w_output[0]

    def forward_item(item):
        rows, row_ids, item_shared, key_ids = item
        return head_forward(rows, row_ids, item_shared, key_ids, own_query, own_output)

    results, kept_queries, kept_attended, kept_totals = lax.map(
        forward_item, (arrived, arrived_ids, all_shared, all_ids)
    )
    returned = lax.all_to_all(results, "expert", split_axis=0, concat_axis=0, tiled=True)
    returned_rows = (
        returned.reshape(experts * capacity, width)[slot_index]
        .astype(jnp.float32)
        .reshape(length, choose, width)
    )
    mixed = jnp.sum(gates[:, :, None] * returned_rows, axis=1)
    hidden_in = inputs + mixed
    normed_two, norm_two, inverse_two = layer_norm_parts(hidden_in, ln_ffn)
    normed_two_low = normed_two.astype(jnp.bfloat16)
    before = product(normed_two_low, w_in)
    activated = gelu_exact(before).astype(jnp.bfloat16)
    output = (hidden_in + product(activated, w_out)).astype(jnp.bfloat16)
    out_weight_grad = product_tn(activated, out_grad)
    activated_grad = product_nt(out_grad, w_out)
    before_grad = (activated_grad * gelu_slope(before)).astype(jnp.bfloat16)
    in_weight_grad = product_tn(normed_two_low, before_grad)
    normed_two_grad = product_nt(before_grad, w_in)
    hidden_back, ln_ffn_grad = layer_norm_back(normed_two_grad, norm_two, inverse_two, ln_ffn)
    hidden_grad = out_grad.astype(jnp.float32) + hidden_back
    gate_grad = jnp.sum(hidden_grad[:, None, :] * returned_rows, axis=2)
    picked_grad = gates * (gate_grad - jnp.sum(gates * gate_grad, axis=-1, keepdims=True))
    logits_grad = jnp.sum(selector * picked_grad[:, :, None], axis=1).astype(jnp.bfloat16)
    router_grad = product_tn(normed_low, logits_grad)
    route_grad = (
        (gates[:, :, None] * hidden_grad[:, None, :])
        .astype(jnp.bfloat16)
        .reshape(length * choose, width)
    )
    route_dispatch = (
        jnp.zeros((experts * capacity, width), jnp.bfloat16)
        .at[slot_index]
        .set(route_grad)
        .reshape(experts, capacity, width)
    )
    arrived_grad = lax.all_to_all(route_dispatch, "expert", split_axis=0, concat_axis=0, tiled=True)

    def backward_item(item):
        rows, row_ids, item_shared, key_ids, queries, attended, totals, result_grad = item
        return head_backward(
            rows,
            row_ids,
            item_shared,
            key_ids,
            own_query,
            own_output,
            queries,
            attended,
            totals,
            result_grad,
        )

    rows_grad, shared_parts, query_parts, output_parts = lax.map(
        backward_item,
        (
            arrived,
            arrived_ids,
            all_shared,
            all_ids,
            kept_queries,
            kept_attended,
            kept_totals,
            arrived_grad,
        ),
    )
    back_rows = lax.all_to_all(rows_grad, "expert", split_axis=0, concat_axis=0, tiled=True)
    shared_grad = lax.psum_scatter(
        shared_parts.reshape(experts * length, 2 * head_size).astype(jnp.bfloat16),
        "expert",
        scatter_dimension=0,
        tiled=True,
    )
    query_grad_sum = jnp.sum(query_parts, axis=0)[None]
    output_grad_sum = jnp.sum(output_parts, axis=0)[None]
    query_total, output_total = (
        lax.psum(query_grad_sum.astype(jnp.bfloat16), ("dp", "tok")).astype(jnp.float32),
        lax.psum(output_grad_sum.astype(jnp.bfloat16), ("dp", "tok")).astype(jnp.float32),
    )
    kv_weight_grad = product_tn(normed_low, shared_grad)
    routes_back = (
        back_rows.reshape(experts * capacity, width)[slot_index]
        .astype(jnp.float32)
        .reshape(length, choose, width)
    )
    normed_grad = (
        product_nt(shared_grad, w_kv)
        + product_nt(logits_grad, w_router)
        + jnp.sum(routes_back, axis=1)
    )
    input_back, ln_attn_grad = layer_norm_back(normed_grad, norm_one, inverse_one, ln_attn)
    input_grad = (hidden_grad + input_back).astype(jnp.bfloat16)
    summed = lax.psum(
        (ln_attn_grad, kv_weight_grad, router_grad, in_weight_grad, out_weight_grad, ln_ffn_grad),
        ("dp", "expert", "tok"),
    )
    return (
        output,
        input_grad,
        summed[0],
        summed[1],
        summed[2],
        query_total,
        output_total,
        summed[5],
        summed[3],
        summed[4],
    )


def solution(mesh):
    return jax.shard_map(
        body,
        mesh=mesh,
        in_specs=(
            P(("dp", "expert", "tok"), None),
            P(("dp", "expert", "tok"), None),
            P(("dp", "expert", "tok"), None),
            P(("dp", "expert", "tok"), None),
            P(),
            P(),
            P(),
            P("expert", None, None),
            P("expert", None, None),
            P(),
            P(),
            P(),
        ),
        out_specs=(
            P(("dp", "expert", "tok"), None),
            P(("dp", "expert", "tok"), None),
            P(),
            P(),
            P(),
            P("expert", None, None),
            P("expert", None, None),
            P(),
            P(),
            P(),
        ),
        check_vma=False,
    )
```

profile of v0, /device:TPU:0, one launch (start us, length us, event | category | flops | bytes accessed | tf_op | source)
XLA Modules:
  0.0 818.5 jit_solution(17089918963078222424)
XLA Ops:
  19.5 8.6 %scatter_custom_fusion = s32[3072]{0:T(1024)} fusion(s32[2048]{0:T(1024)S(1)} %bitcast.203, s32[2048]{0:T(1024)S(1)} %reshape.331, s32[]{:T(128)} %constant.101.clone.1), kind=kCustom, calls=%fused_computation.137 | custom fusion | bytes 12292 | tf_op jit(solution)/shard_map/scatter | solution.py:149
  28.2 6.3 all-to-all-start
  37.6 2.4 broadcast_in_dim.56
  40.0 4.1 reshape.339
  44.1 12.1 %scatter_custom_fusion.1 = bf16[3072,512]{1,0:T(8,128)(2,1)} fusion(s32[2048]{0:T(1024)S(1)} %bitcast.204, bf16[2048,512]{1,0:T(8,128)(2,1)} %reshape.339, bf16[]{:T(256)} %constant.98.clone.1), kind=kCustom, calls=%fused_computation.115 | custom fusion | bytes 3146240 | tf_op jit(solution)/shard_map/scatter | solution.py:143
  56.1 5.2 all-to-all-start.1
  62.6 91.3 %all-gather = s32[1,4096]{1,0:T(1,128)S(1)} all-gather(s32[1,1024]{1,0:T(1,128)S(1)} %copy-done.35), channel_id=2, replica_groups=mesh['dp'=4,'expert'=4,'tok'=2] {'expert'}, dimensions={1}, use_global_device_ids=true | all-gather | bytes 20480 | tf_op jit(solution)/shard_map/all_gather | solution.py:158
  157.8 41.3 %while.32 = (s32[]{:T(128)}, bf16[4,768,512]{2,1,0:T(8,128)(2,1)}, bf16[4,768,64]{1,2,0:T(8,128)(2,1)}, bf16[4,768,64]{1,2,0:T(8,128)(2,1)}, f32[4,768]{1,0:T(4,...) while((s32[]{:T(128)}, bf16[4,768,512]{2,1,0:T(8,128)(2,1)}, ...), condition=%wide.region_13.14_spmd, body=%wide.region_10.13_spmd.sunk | while | flops 314277120 | bytes 12918941 | solution.py:169
  169.1 2.2 bitcast_dynamic-update-slice_fusion.4
  189.8 2.2 bitcast_dynamic-update-slice_fusion.4
  199.1 4.8 all-to-all-start.2
  204.9 66.7 %all-to-all-done.2 = bf16[4,768,512]{2,1,0:T(8,128)(2,1)} async-done(((bf16[4,768,512]{2,1,0:T(8,128)(2,1)}), bf16[4,768,512]{2,1,0:T(8,128)(2,1)}, u32[]{:S(2)}, u32[]{:S(2)}) %all-to-all-start.2) | async-done | bytes 3145760 | tf_op jit(solution)/shard_map/all_to_all | solution.py:172
  271.6 11.6 %gather_fusion = bf16[2048,512]{1,0:T(8,128)(2,1)} fusion(bf16[3072,512]{1,0:T(8,128)(2,1)} %bitcast.25, s32[2048]{0:T(1024)S(1)} %broadcast_clamp_fusion), kind=kCustom, calls=%fused_computation | custom fusion | bytes 4202496 | tf_op jit(solution)/shard_map/gather | solution.py:174
  283.2 5.4 reshape.309
  288.6 7.7 multiply_reduce_fusion.2
  297.1 4.7 multiply_convert_fusion.1
  301.8 5.0 fusion.47
  306.9 3.4 multiply_reduce_fusion.3
  312.8 3.4 mul.256
  316.2 6.2 mul.257
  322.5 13.1 %scatter_custom_fusion.2 = bf16[3072,512]{1,0:T(8,128)(2,1)} fusion(s32[2048]{0:T(1024)S(1)} %bitcast.206, f32[2048,512]{1,0:T(8,128)} %mul.257, f32[2048]{0:T(1024)S(1)} %div.59, bf16[]{:T(256)} %constant.98.clone.1), kind=kCustom, calls=%fused_computation.102 | custom fusion | flops 2097152 | bytes 7348226 | tf_op jit(solution)/shard_map/scatter | solution.py:204
  335.6 3.7 all-to-all-start.3
  339.4 70.0 %all-to-all-done.3 = bf16[4,768,512]{2,1,0:T(8,128)(2,1)S(1)} async-done(((bf16[4,768,512]{2,1,0:T(8,128)(2,1)}), bf16[4,768,512]{2,1,0:T(8,128)(2,1)S(1)}, u32[]{:S(2)}, u32[]{:S(2)}) %all-to-all-start.3) | async-done | bytes 3145760 | tf_op jit(solution)/shard_map/all_to_all | solution.py:207
  411.3 68.2 %while.33 = (s32[]{:T(128)}, bf16[4,768,512]{2,1,0:T(8,128)(2,1)}, bf16[4,1024,128]{2,1,0:T(8,128)(2,1)}, f32[4,512,64]{1,2,0:T(8,128)}, f32[4,64,512]{2,1,0:T(8...) while((s32[]{:T(128)}, bf16[4,768,512]{2,1,0:T(8,128)(2,1)}, ...), condition=%wide.region_22.23_spmd, body=%wide.region_20.22_spmd.sunk | while | flops 713702656 | bytes 31267520 | solution.py:224
  416.7 2.2 multiply_reduce_fusion.10
  426.2 2.2 fusion.174
  433.8 2.2 multiply_reduce_fusion.10
  443.3 2.2 fusion.174
  450.9 2.2 multiply_reduce_fusion.10
  460.3 2.2 fusion.174
  467.9 2.2 multiply_reduce_fusion.10
  477.4 2.2 fusion.174
  479.6 3.7 all-to-all-start.4
  483.8 7.2 fusion.84
  491.0 4.6 fusion.78
  499.1 30.9 %reduce-scatter.2.cloned.1.call-done = bf16[1024,128]{1,0:T(8,128)(2,1)} async-done(((bf16[4096,128]{1,0:T(8,128)(2,1)}), bf16[1024,128]{1,0:T(8,128)(2,1)}) %reduce-scatter.2.cloned.1.call-update) | async-done | bytes 262160 | tf_op jit(solution)/shard_map/reduce_scatter | solution.py:238
  530.0 2.4 fusion.83
  532.5 5.9 multiply_reduce_fusion.1
  541.8 6.8 add_convert_fusion
  548.6 64.8 %all-reduce.8.cloned.1.call-done = (bf16[1,512,64]{1,2,0:T(8,128)(2,1)}, bf16[1,64,512]{2,1,0:T(8,128)(2,1)}) async-done(((bf16[1,512,64]{1,2,0:T(8,128)(2,1)}, bf16[1,64,512]{2,1,0:T(8,128)(2,1)}), (bf16[1,512,64]{1,2,0:T(8,128)(2,1)}, bf16[1,64,512]{2,1,0:T(8,128)(2,1)})) %all-reduce.8.cloned.1.call-update) | async-done | bytes 131088 | tf_op jit(solution)/shard_map/psum | solution.py:247
  618.2 9.4 %gather_fusion.1 = bf16[2048,512]{1,0:T(8,128)(2,1)} fusion(bf16[3072,512]{1,0:T(8,128)(2,1)S(1)} %bitcast.191, s32[2048]{0:T(1024)S(1)} %copy-done.22), kind=kCustom, calls=%fused_computation.1 | custom fusion | bytes 4202496 | tf_op jit(solution)/shard_map/gather | solution.py:252
  627.6 5.5 reshape.310
  633.1 8.7 %reduce_sum.214 = f32[1024,512]{1,0:T(8,128)} reduce(f32[1024,2,512]{2,1,0:T(2,128)} %reshape.310, f32[]{:T(128)} %constant.71.clone.1), dimensions={1}, to_apply=%region_27.28 | reduce | flops 524288 | bytes 6291460 | tf_op jit(solution)/shard_map/reduce_sum | solution.py:259
  641.9 4.8 fusion.60
  646.7 40.1 %all-reduce = (f32[512]{0:T(512)}, f32[512,4]{0,1:T(4,128)}, f32[512]{0:T(512)}) all-reduce(f32[512]{0:T(512)S(1)} %get-tuple-element.235, f32[512,4]{0,1:T(4,128)S(1)} %copy-done.28, f32[512]{0:T(512)S(1)} %copy-done.36), channel_id=1, replica_groups=mesh['dp'=4,'expert'=4,'tok'=2] {'dp','expert','tok'}, use_global_device_ids=true, to_apply=%region_31.32 | all-reduce | flops 3072 | bytes 24576 | tf_op jit(solution)/shard_map/psum | solution.py:263
  686.8 3.0 fusion.59
  689.9 113.4 %all-reduce.6.cloned.1.call-done = (f32[512,128]{1,0:T(8,128)}, f32[512,2048]{1,0:T(8,128)}, f32[2048,512]{1,0:T(8,128)}) async-done(((f32[512,128]{1,0:T(8,128)}, f32[512,2048]{1,0:T(8,128)}, f32[2048,512]{1,0:T(8,128)}), (f32[512,128]{1,0:T(8,128)}, f32[512,2048]{1,0:T(8,128)}, f32[2048,512]{1,0:T(8,128)})) %all-reduce.6.cloned.1.call-update) | async-done | bytes 8650768 | tf_op jit(solution)/shard_map/psum | solution.py:263
  805.0 4.8 copy.166
  (252 shorter events, 129.9 us)
Async XLA Ops:
  7.2 289.8 %copy-start = (bf16[512,2048]{1,0:T(8,128)(2,1)S(1)}, bf16[512,2048]{1,0:T(8,128)(2,1)}, u32[]{:S(2)}) copy-start(bf16[512,2048]{1,0:T(8,128)(2,1)} %param.26) | copy-start | bytes 6291460
  7.2 27.3 %copy-start.5 = (bf16[1024,512]{1,0:T(8,128)(2,1)S(1)}, bf16[1024,512]{1,0:T(8,128)(2,1)}, u32[]{:S(2)}) copy-start(bf16[1024,512]{1,0:T(8,128)(2,1)} %param.16) | copy-start | bytes 3145732
  7.2 28.7 %copy-start.29 = (f32[512]{0:T(512)S(1)}, f32[512]{0:T(512)}, u32[]{:S(2)}) copy-start(f32[512]{0:T(512)} %param.20) | copy-start | bytes 6148
  28.2 28.0 %all-to-all-start = ((s32[4,1,768]{2,1,0:T(1,128)}), s32[4,1,768]{2,1,0:T(1,128)S(1)}, u32[]{:S(2)}, u32[]{:S(2)}) async-start(s32[4,1,768]{2,1,0:T(1,128)} %bitcast.20), calls=%async_computation | async-start | bytes 24576 | tf_op jit(solution)/shard_map/all_to_all | solution.py:154
  34.7 0.6 copy-start.19
  35.3 0.6 copy-start.23
  37.5 166.3 %copy-start.4 = (bf16[1024,512]{1,0:T(8,128)(2,1)}, bf16[1024,512]{1,0:T(8,128)(2,1)S(1)}, u32[]{:S(2)}) copy-start(bf16[1024,512]{1,0:T(8,128)(2,1)S(1)} %fusion.54) | copy-start | bytes 3145732
  56.1 5.3 copy-start.15
  56.1 6.4 copy-start.35
  56.1 99.0 %copy-start.25 = (bf16[1,512,64]{1,2,0:T(8,128)(2,1)S(1)}, bf16[1,512,64]{1,2,0:T(8,128)(2,1)}, u32[]{:S(2)}) copy-start(bf16[1,512,64]{1,2,0:T(8,128)(2,1)} %param.23) | copy-start | bytes 196612
  56.1 99.7 %all-to-all-start.1 = ((bf16[4,768,512]{2,1,0:T(8,128)(2,1)}), bf16[4,768,512]{2,1,0:T(8,128)(2,1)}, u32[]{:S(2)}, u32[]{:S(2)}) async-start(bf16[4,768,512]{2,1,0:T(8,128)(2,1)} %bitcast.192), calls=%async_computation.1 | async-start | bytes 6291456 | tf_op jit(solution)/shard_map/all_to_all | solution.py:153
  61.4 94.5 %all-gather.3.cloned.1.call-start = ((), (), s32[]{:S(2)}) async-start(), calls=%async_computation.6 | async-start | bytes 1310720 | tf_op jit(solution)/shard_map/all_gather | solution.py:157
  199.1 4.8 copy-start.33
  199.1 5.2 copy-start.17
  199.1 72.5 %all-to-all-start.2 = ((bf16[4,768,512]{2,1,0:T(8,128)(2,1)}), bf16[4,768,512]{2,1,0:T(8,128)(2,1)}, u32[]{:S(2)}, u32[]{:S(2)}) async-start(bf16[4,768,512]{2,1,0:T(8,128)(2,1)} %get-tuple-element.150), calls=%async_computation.2 | async-start | bytes 6291456 | tf_op jit(solution)/shard_map/all_to_all | solution.py:172
  204.4 78.8 %copy-start.26 = (f32[1024]{0:T(1024)}, f32[1024]{0:T(1024)S(1)}, u32[]{:S(2)}) copy-start(f32[1024]{0:T(1024)S(1)} %fusion.74) | copy-start | bytes 12292
  204.9 78.2 %copy-start.21 = (s32[2048]{0:T(1024)}, s32[2048]{0:T(1024)S(1)}, u32[]{:S(2)}) copy-start(s32[2048]{0:T(1024)S(1)} %broadcast_clamp_fusion) | copy-start | bytes 24580
  288.6 7.7 copy-start.6
  296.3 0.8 copy-start.31
  296.6 13.7 %copy-start.2 = (f32[1024,512]{1,0:T(8,128)}, f32[1024,512]{1,0:T(8,128)S(1)}, u32[]{:S(2)}) copy-start(f32[1024,512]{1,0:T(8,128)S(1)} %get-tuple-element.300) | copy-start | bytes 6291460
  297.0 4.8 copy-start.14
  297.1 4.7 copy-start.37
  306.9 3.4 copy-start.10
  311.4 1.4 copy-start.8
  335.6 73.8 %all-to-all-start.3 = ((bf16[4,768,512]{2,1,0:T(8,128)(2,1)}), bf16[4,768,512]{2,1,0:T(8,128)(2,1)S(1)}, u32[]{:S(2)}, u32[]{:S(2)}) async-start(bf16[4,768,512]{2,1,0:T(8,128)(2,1)} %bitcast.193), calls=%async_computation.3 | async-start | bytes 6291456 | tf_op jit(solution)/shard_map/all_to_all | solution.py:207
  339.3 190.7 %reduce-scatter.2.cloned.1.call-start = ((), (), s32[]{:S(2)}) async-start(), calls=%async_computation.7 | async-start | bytes 1310720 | tf_op jit(solution)/shard_map/reduce_scatter | solution.py:238
  479.6 138.6 %all-to-all-start.4 = ((bf16[4,768,512]{2,1,0:T(8,128)(2,1)}), bf16[4,768,512]{2,1,0:T(8,128)(2,1)S(1)}, u32[]{:S(2)}, u32[]{:S(2)}) async-start(bf16[4,768,512]{2,1,0:T(8,128)(2,1)} %get-tuple-element.155), calls=%async_computation.5 | async-start | bytes 6291456 | tf_op jit(solution)/shard_map/all_to_all | solution.py:237
  483.3 130.1 %all-reduce.8.cloned.1.call-start = ((), (), s32[]{:S(2)}) async-start(), calls=%async_computation.9 | async-start | bytes 262144 | tf_op jit(solution)/shard_map/psum | solution.py:247
  483.8 7.2 copy-start.3
  483.8 7.2 copy-start.11
  483.8 7.2 copy-start.32
  499.0 304.3 %all-reduce.6.cloned.1.call-start = ((), (), s32[]{:S(2)}) async-start(), calls=%async_computation.8 | async-start | bytes 17301504 | tf_op jit(solution)/shard_map/psum | solution.py:263
  532.4 7.2 copy-start.27
  532.4 7.2 copy-start.18
  541.8 74.6 %copy-start.13 = (bf16[1024,128]{1,0:T(8,128)(2,1)S(1)}, bf16[1024,128]{1,0:T(8,128)(2,1)}, u32[]{:S(2)}) copy-start(bf16[1024,128]{1,0:T(8,128)(2,1)} %reduce-scatter.2.cloned.1.call-done) | copy-start | bytes 786436
  541.8 74.6 %copy-start.16 = (bf16[512,128]{1,0:T(8,128)(2,1)S(1)}, bf16[512,128]{1,0:T(8,128)(2,1)}, u32[]{:S(2)}) copy-start(bf16[512,128]{1,0:T(8,128)(2,1)} %param.21) | copy-start | bytes 393220
  541.8 76.4 %copy-start.22 = (s32[2048]{0:T(1024)S(1)}, s32[2048]{0:T(1024)}, u32[]{:S(2)}) copy-start(s32[2048]{0:T(1024)} %copy-done.21) | copy-start | bytes 24580
  633.1 8.7 %copy-start.7 = (bf16[1024,512]{1,0:T(8,128)(2,1)S(1)}, bf16[1024,512]{1,0:T(8,128)(2,1)}, u32[]{:S(2)}) copy-start(bf16[1024,512]{1,0:T(8,128)(2,1)} %param.16) | copy-start | bytes 3145732
  633.1 8.7 %copy-start.20 = (f32[1024]{0:T(1024)S(1)}, f32[1024]{0:T(1024)}, u32[]{:S(2)}) copy-start(f32[1024]{0:T(1024)} %copy-done.19) | copy-start | bytes 12292
  633.1 8.7 %copy-start.24 = (f32[1024]{0:T(1024)S(1)}, f32[1024]{0:T(1024)}, u32[]{:S(2)}) copy-start(f32[1024]{0:T(1024)} %copy-done.23) | copy-start | bytes 12292
  633.1 8.7 %copy-start.30 = (f32[512]{0:T(512)S(1)}, f32[512]{0:T(512)}, u32[]{:S(2)}) copy-start(f32[512]{0:T(512)} %param.20) | copy-start | bytes 6148
  633.1 8.7 %copy-start.34 = (bf16[512,4]{0,1:T(4,128)(2,1)S(1)}, bf16[512,4]{0,1:T(4,128)(2,1)}, u32[]{:S(2)}) copy-start(bf16[512,4]{0,1:T(4,128)(2,1)} %param.22) | copy-start | bytes 12292
  641.8 4.9 copy-start.28
  641.8 4.9 copy-start.36
  641.9 45.0 %copy-start.9 = (f32[1024,512]{1,0:T(8,128)S(1)}, f32[1024,512]{1,0:T(8,128)}, u32[]{:S(2)}) copy-start(f32[1024,512]{1,0:T(8,128)} %copy-done.8) | copy-start | bytes 6291460
  805.0 4.9 copy-start.12
  805.0 6.9 copy-start.1
Sparse Core Ops, SparseCore 0:
  64.3 43.4 all-gather.2
  479.7 50.2 reduce-scatter.1
  533.9 79.4 all-reduce.7
  620.0 183.2 all-reduce.5
where the time goes:
time: 829 us; the launch traced here: 819 us
  waiting for transfers between devices  346 us (42%)
  blocking collectives  131 us (16%)
  matrix products  122 us (15%)
  local copies, waits for them, and re-layouts  120 us (14%)
  other arithmetic  60.4 us (7%)
  starting transfers between devices  24.3 us (3%)
  between operations  14.5 us (2%)
    psum x1, waiting for transfers between devices, body(): lax.psum((ln_attn_grad, kv_weight_grad, router_grad, in_weight_grad, out_...  113 us
    all_gather x1, blocking collectives, body(): lax.all_gather(sentence, 'expert', axis=0, tiled=True)  91.3 us
    all_to_all x1, waiting for transfers between devices, body(): lax.all_to_all(route_dispatch, 'expert', split_axis=0, concat_axis=0, til...  70 us
    all_to_all x1, waiting for transfers between devices, body(): lax.all_to_all(results, 'expert', split_axis=0, concat_axis=0, tiled=True)  66.7 us
    psum x1, waiting for transfers between devices, body(): lax.psum(query_grad_sum.astype(jnp.bfloat16), ('dp', 'tok'))  64.8 us
    dot_general x24, matrix products, product_nt(): lax.dot_general(left, right, (((1,), (1,)), ((), ())), preferred_element_...  43.4 us
    dot_general x20, matrix products, product(): return jnp.dot(left, right, preferred_element_type=jnp.float32)  40.2 us
    psum x1, blocking collectives, body(): lax.psum((ln_attn_grad, kv_weight_grad, router_grad, in_weight_grad, out_...  40.1 us
  transfers between devices with their start and end apart: 9, of which 5 were waited for; matrix products, arithmetic and copies ran while one was open for 12% of the time, Pallas kernels for 0%

commit v1 on v0

--- a/solution.py
+++ b/solution.py
@@ -261,8 +261,18 @@
     input_back, ln_attn_grad = layer_norm_back(normed_grad, norm_one, inverse_one, ln_attn)
     input_grad = (hidden_grad + input_back).astype(jnp.bfloat16)
     summed = lax.psum(
-        (ln_attn_grad, kv_weight_grad, router_grad, in_weight_grad, out_weight_grad, ln_ffn_grad),
-        ("dp", "expert", "tok"),
+        lax.psum(
+            (
+                ln_attn_grad,
+                kv_weight_grad,
+                router_grad,
+                in_weight_grad,
+                out_weight_grad,
+                ln_ffn_grad,
+            ),
+            axis_name=("expert", "tok"),
+        ),
+        axis_name="dp",
     )
     return (
         output,

time: 829 us -> 953 us (1.15)
  waiting for transfers between devices: 346 us -> 468 us
    psum x0 -> x1, waiting for transfers between devices: none -> 88.3 us  [body(): lax.psum(lax.psum((ln_attn_grad, kv_weight_grad, router_grad, in_weight_g...]
    psum x1, waiting for transfers between devices: 113 us -> 179 us  [body(): lax.psum((ln_attn_grad, kv_weight_grad, router_grad, in_weight_grad, out_...]
    psum x1, waiting for transfers between devices: 64.8 us -> 37 us  [body(): lax.psum(query_grad_sum.astype(jnp.bfloat16), ('dp', 'tok'))]
    psum x0 -> x1, blocking collectives: none -> 17.2 us  [body(): lax.psum(lax.psum((ln_attn_grad, kv_weight_grad, router_grad, in_weight_g...]
    reduce_scatter x1, waiting for transfers between devices: 30.9 us -> 14.3 us  [body(): lax.psum_scatter(shared_parts.reshape(experts * length, 2 * head_size).as...]
    psum x1, blocking collectives: 40.1 us -> 26.2 us  [body(): lax.psum((ln_attn_grad, kv_weight_grad, router_grad, in_weight_grad, out_...]
    all_to_all x1, waiting for transfers between devices: 0.01 us -> 12.8 us  [body(): lax.all_to_all(rows_grad, 'expert', split_axis=0, concat_axis=0, tiled=True)]
  transfers between devices with their start and end apart: 9 -> 10, of which waited for: 5 -> 7; matrix products, arithmetic and copies ran while one was open for 12% -> 10% of each run, Pallas kernels for 0% -> 0%
where the time goes in v1:
time: 953 us; the launch traced here: 942 us
  waiting for transfers between devices  468 us (49%)
  blocking collectives  135 us (14%)
  local copies, waits for them, and re-layouts  121 us (13%)
  matrix products  121 us (13%)
  other arithmetic  58.1 us (6%)
  starting transfers between devices  24.4 us (3%)
  between operations  14.6 us (2%)
    psum x1, waiting for transfers between devices, body(): lax.psum((ln_attn_grad, kv_weight_grad, router_grad, in_weight_grad, out_...  179 us
    all_gather x1, blocking collectives, body(): lax.all_gather(sentence, 'expert', axis=0, tiled=True)  91.3 us
    psum x1, waiting for transfers between devices, body(): lax.psum(lax.psum((ln_attn_grad, kv_weight_grad, router_grad, in_weight_g...  88.3 us
    all_to_all x1, waiting for transfers between devices, body(): lax.all_to_all(route_dispatch, 'expert', split_axis=0, concat_axis=0, til...  70 us
    all_to_all x1, waiting for transfers between devices, body(): lax.all_to_all(results, 'expert', split_axis=0, concat_axis=0, tiled=True)  66.7 us
    dot_general x24, matrix products, product_nt(): lax.dot_general(left, right, (((1,), (1,)), ((), ())), preferred_element_...  43.2 us
    dot_general x20, matrix products, product(): return jnp.dot(left, right, preferred_element_type=jnp.float32)  40.2 us
    dot_general x20, matrix products, product_tn(): lax.dot_general(left, right, (((0,), (0,)), ((), ())), preferred_element_...  37.9 us
  transfers between devices with their start and end apart: 10, of which 7 were waited for; matrix products, arithmetic and copies ran while one was open for 10% of the time, Pallas kernels for 0%

profile of v1, /device:TPU:0, one launch (start us, length us, event | category | flops | bytes accessed | tf_op | source)
XLA Modules:
  0.0 942.1 jit_solution(14380365934967802000)
XLA Ops:
  19.5 8.6 scatter_custom_fusion
  28.2 6.3 all-to-all-start
  37.6 2.4 broadcast_in_dim.56
  40.0 4.1 reshape.339
  44.1 12.1 %scatter_custom_fusion.1 = bf16[3072,512]{1,0:T(8,128)(2,1)} fusion(s32[2048]{0:T(1024)S(1)} %bitcast.204, bf16[2048,512]{1,0:T(8,128)(2,1)} %reshape.339, bf16[]{:T(256)} %constant.98.clone.1), kind=kCustom, calls=%fused_computation.115 | custom fusion | bytes 3146240 | tf_op jit(solution)/shard_map/scatter | solution.py:143
  56.1 5.2 all-to-all-start.1
  62.6 91.3 %all-gather = s32[1,4096]{1,0:T(1,128)S(1)} all-gather(s32[1,1024]{1,0:T(1,128)S(1)} %copy-done.38), channel_id=2, replica_groups=mesh['dp'=4,'expert'=4,'tok'=2] {'expert'}, dimensions={1}, use_global_device_ids=true | all-gather | bytes 20480 | tf_op jit(solution)/shard_map/all_gather | solution.py:158
  157.8 41.3 %while.32 = (s32[]{:T(128)}, bf16[4,768,512]{2,1,0:T(8,128)(2,1)}, bf16[4,768,64]{1,2,0:T(8,128)(2,1)}, bf16[4,768,64]{1,2,0:T(8,128)(2,1)}, f32[4,768]{1,0:T(4,...) while((s32[]{:T(128)}, bf16[4,768,512]{2,1,0:T(8,128)(2,1)}, ...), condition=%wide.region_13.14_spmd, body=%wide.region_10.13_spmd.sunk | while | flops 314277120 | bytes 12918941 | solution.py:169
  199.1 4.8 all-to-all-start.2
  205.0 66.7 %all-to-all-done.2 = bf16[4,768,512]{2,1,0:T(8,128)(2,1)} async-done(((bf16[4,768,512]{2,1,0:T(8,128)(2,1)}), bf16[4,768,512]{2,1,0:T(8,128)(2,1)}, u32[]{:S(2)}, u32[]{:S(2)}) %all-to-all-start.2) | async-done | bytes 3145760 | tf_op jit(solution)/shard_map/all_to_all | solution.py:172
  271.6 11.6 %gather_fusion = bf16[2048,512]{1,0:T(8,128)(2,1)} fusion(bf16[3072,512]{1,0:T(8,128)(2,1)} %bitcast.25, s32[2048]{0:T(1024)S(1)} %broadcast_clamp_fusion), kind=kCustom, calls=%fused_computation | custom fusion | bytes 4202496 | tf_op jit(solution)/shard_map/gather | solution.py:174
  283.2 5.4 reshape.309
  288.6 7.7 multiply_reduce_fusion.2
  297.1 4.7 multiply_convert_fusion.1
  301.8 5.0 fusion.47
  306.9 3.3 multiply_reduce_fusion.3
  312.8 3.4 mul.256
  316.2 6.2 mul.257
  322.5 13.1 %scatter_custom_fusion.2 = bf16[3072,512]{1,0:T(8,128)(2,1)} fusion(s32[2048]{0:T(1024)S(1)} %bitcast.206, f32[2048,512]{1,0:T(8,128)} %mul.257, f32[2048]{0:T(1024)S(1)} %div.59, bf16[]{:T(256)} %constant.98.clone.1), kind=kCustom, calls=%fused_computation.102 | custom fusion | flops 2097152 | bytes 7348226 | tf_op jit(solution)/shard_map/scatter | solution.py:204
  335.6 3.7 all-to-all-start.3
  339.4 70.0 %all-to-all-done.3 = bf16[4,768,512]{2,1,0:T(8,128)(2,1)S(1)} async-done(((bf16[4,768,512]{2,1,0:T(8,128)(2,1)}), bf16[4,768,512]{2,1,0:T(8,128)(2,1)S(1)}, u32[]{:S(2)}, u32[]{:S(2)}) %all-to-all-start.3) | async-done | bytes 3145760 | tf_op jit(solution)/shard_map/all_to_all | solution.py:207
  411.4 68.3 %while.33 = (s32[]{:T(128)}, bf16[4,768,512]{2,1,0:T(8,128)(2,1)}, bf16[4,1024,128]{2,1,0:T(8,128)(2,1)}, f32[4,512,64]{1,2,0:T(8,128)}, f32[4,64,512]{2,1,0:T(8...) while((s32[]{:T(128)}, bf16[4,768,512]{2,1,0:T(8,128)(2,1)}, ...), condition=%wide.region_22.23_spmd, body=%wide.region_20.22_spmd.sunk | while | flops 713702656 | bytes 31267520 | solution.py:224
  416.8 2.2 multiply_reduce_fusion.10
  426.2 2.2 fusion.174
  433.8 2.2 multiply_reduce_fusion.10
  443.3 2.2 fusion.174
  450.9 2.2 multiply_reduce_fusion.10
  460.4 2.2 fusion.174
  468.0 2.2 multiply_reduce_fusion.10
  477.4 2.2 fusion.174
  480.1 7.0 fusion.84
  487.2 4.6 fusion.78
  491.8 14.3 %reduce-scatter.2.cloned.1.call-done = bf16[1024,128]{1,0:T(8,128)(2,1)} async-done(((bf16[4096,128]{1,0:T(8,128)(2,1)}), bf16[1024,128]{1,0:T(8,128)(2,1)}) %reduce-scatter.2.cloned.1.call-update) | async-done | bytes 262160 | tf_op jit(solution)/shard_map/reduce_scatter | solution.py:238
  510.6 178.7 %all-reduce.9.cloned.1.call-done = (f32[512,128]{1,0:T(8,128)}, f32[512,2048]{1,0:T(8,128)}, f32[2048,512]{1,0:T(8,128)}) async-done(((f32[512,128]{1,0:T(8,128)}, f32[512,2048]{1,0:T(8,128)}, f32[2048,512]{1,0:T(8,128)}), (f32[512,128]{1,0:T(8,128)}, f32[512,2048]{1,0:T(8,128)}, f32[2048,512]{1,0:T(8,128)})) %all-reduce.9.cloned.1.call-update) | async-done | bytes 8650768 | tf_op jit(solution)/shard_map/psum | solution.py:264
  689.4 3.8 all-to-all-start.4
  693.2 5.9 multiply_reduce_fusion.1
  702.5 6.8 add_convert_fusion
  709.3 37.0 %all-reduce.13.cloned.1.call-done = (bf16[1,512,64]{1,2,0:T(8,128)(2,1)}, bf16[1,64,512]{2,1,0:T(8,128)(2,1)}) async-done(((bf16[1,512,64]{1,2,0:T(8,128)(2,1)}, bf16[1,64,512]{2,1,0:T(8,128)(2,1)}), (bf16[1,512,64]{1,2,0:T(8,128)(2,1)}, bf16[1,64,512]{2,1,0:T(8,128)(2,1)})) %all-reduce.13.cloned.1.call-update) | async-done | bytes 131088 | tf_op jit(solution)/shard_map/psum | solution.py:247
  751.1 12.8 %all-to-all-done.4 = bf16[4,768,512]{2,1,0:T(8,128)(2,1)S(1)} async-done(((bf16[4,768,512]{2,1,0:T(8,128)(2,1)}), bf16[4,768,512]{2,1,0:T(8,128)(2,1)S(1)}, u32[]{:S(2)}, u32[]{:S(2)}) %all-to-all-start.4) | async-done | bytes 3145760 | tf_op jit(solution)/shard_map/all_to_all | solution.py:237
  764.0 9.2 gather_fusion.1
  773.2 5.6 reshape.310
  778.8 8.6 reduce_sum.214
  787.5 4.7 fusion.60
  792.2 26.2 %all-reduce = (f32[512]{0:T(512)S(1)}, f32[512,4]{0,1:T(4,128)S(1)}, f32[512]{0:T(512)S(1)}) all-reduce(f32[512]{0:T(512)S(1)} %get-tuple-element.235, f32[512,4]{0,1:T(4,128)S(1)} %copy-done.31, f32[512]{0:T(512)S(1)} %copy-done.39), channel_id=1, replica_groups=mesh['dp'=4,'expert'=4,'tok'=2] {'expert','tok'}, use_global_device_ids=true, to_apply=%region_31.32 | all-reduce | flops 3072 | bytes 24576 | tf_op jit(solution)/shard_map/psum | solution.py:264
  818.4 17.2 %all-reduce.2 = (f32[512]{0:T(512)}, f32[512,4]{0,1:T(4,128)}, f32[512]{0:T(512)}) all-reduce(f32[512]{0:T(512)S(1)} %get-tuple-element.291, f32[512,4]{0,1:T(4,128)S(1)} %get-tuple-element.292, f32[512]{0:T(512)S(1)} %get-tuple-element.293), channel_id=1, replica_groups=mesh['dp'=4,'expert'=4,'tok'=2] {'dp'}, use_global_device_ids=true, to_apply=%region_32.33 | all-reduce | flops 3072 | bytes 24576 | tf_op jit(solution)/shard_map/psum | solution.py:263
  835.5 3.0 fusion.59
  838.6 88.3 %all-reduce.11.cloned.1.call-done = (f32[512,128]{1,0:T(8,128)}, f32[512,2048]{1,0:T(8,128)}, f32[2048,512]{1,0:T(8,128)}) async-done(((f32[512,128]{1,0:T(8,128)}, f32[512,2048]{1,0:T(8,128)}, f32[2048,512]{1,0:T(8,128)}), (f32[512,128]{1,0:T(8,128)}, f32[512,2048]{1,0:T(8,128)}, f32[2048,512]{1,0:T(8,128)})) %all-reduce.11.cloned.1.call-update) | async-done | bytes 8650768 | tf_op jit(solution)/shard_map/psum | solution.py:263
  928.5 4.8 copy.169
  (262 shorter events, 135.3 us)
Async XLA Ops:
  7.2 289.9 %copy-start = (bf16[512,2048]{1,0:T(8,128)(2,1)S(1)}, bf16[512,2048]{1,0:T(8,128)(2,1)}, u32[]{:S(2)}) copy-start(bf16[512,2048]{1,0:T(8,128)(2,1)} %param.26) | copy-start | bytes 6291460
  7.2 27.3 %copy-start.6 = (bf16[1024,512]{1,0:T(8,128)(2,1)S(1)}, bf16[1024,512]{1,0:T(8,128)(2,1)}, u32[]{:S(2)}) copy-start(bf16[1024,512]{1,0:T(8,128)(2,1)} %param.16) | copy-start | bytes 3145732
  7.2 28.7 %copy-start.32 = (f32[512]{0:T(512)S(1)}, f32[512]{0:T(512)}, u32[]{:S(2)}) copy-start(f32[512]{0:T(512)} %param.20) | copy-start | bytes 6148
  28.2 28.0 %all-to-all-start = ((s32[4,1,768]{2,1,0:T(1,128)}), s32[4,1,768]{2,1,0:T(1,128)S(1)}, u32[]{:S(2)}, u32[]{:S(2)}) async-start(s32[4,1,768]{2,1,0:T(1,128)} %bitcast.20), calls=%async_computation | async-start | bytes 24576 | tf_op jit(solution)/shard_map/all_to_all | solution.py:154
  37.5 166.4 %copy-start.4 = (bf16[1024,512]{1,0:T(8,128)(2,1)}, bf16[1024,512]{1,0:T(8,128)(2,1)S(1)}, u32[]{:S(2)}) copy-start(bf16[1024,512]{1,0:T(8,128)(2,1)S(1)} %fusion.54) | copy-start | bytes 3145732
  56.1 5.3 copy-start.18
  56.1 6.4 copy-start.38
  56.1 99.0 %copy-start.28 = (bf16[1,512,64]{1,2,0:T(8,128)(2,1)S(1)}, bf16[1,512,64]{1,2,0:T(8,128)(2,1)}, u32[]{:S(2)}) copy-start(bf16[1,512,64]{1,2,0:T(8,128)(2,1)} %param.23) | copy-start | bytes 196612
  56.1 99.7 %all-to-all-start.1 = ((bf16[4,768,512]{2,1,0:T(8,128)(2,1)}), bf16[4,768,512]{2,1,0:T(8,128)(2,1)}, u32[]{:S(2)}, u32[]{:S(2)}) async-start(bf16[4,768,512]{2,1,0:T(8,128)(2,1)} %bitcast.192), calls=%async_computation.1 | async-start | bytes 6291456 | tf_op jit(solution)/shard_map/all_to_all | solution.py:153
  61.4 94.5 %all-gather.3.cloned.1.call-start = ((), (), s32[]{:S(2)}) async-start(), calls=%async_computation.6 | async-start | bytes 1310720 | tf_op jit(solution)/shard_map/all_gather | solution.py:157
  199.1 4.8 copy-start.36
  199.1 5.2 copy-start.20
  199.1 72.5 %all-to-all-start.2 = ((bf16[4,768,512]{2,1,0:T(8,128)(2,1)}), bf16[4,768,512]{2,1,0:T(8,128)(2,1)}, u32[]{:S(2)}, u32[]{:S(2)}) async-start(bf16[4,768,512]{2,1,0:T(8,128)(2,1)} %get-tuple-element.150), calls=%async_computation.2 | async-start | bytes 6291456 | tf_op jit(solution)/shard_map/all_to_all | solution.py:172
  204.4 78.8 %copy-start.29 = (f32[1024]{0:T(1024)}, f32[1024]{0:T(1024)S(1)}, u32[]{:S(2)}) copy-start(f32[1024]{0:T(1024)S(1)} %fusion.74) | copy-start | bytes 12292
  204.9 78.3 %copy-start.24 = (s32[2048]{0:T(1024)}, s32[2048]{0:T(1024)S(1)}, u32[]{:S(2)}) copy-start(s32[2048]{0:T(1024)S(1)} %broadcast_clamp_fusion) | copy-start | bytes 24580
  288.6 7.7 copy-start.7
  296.6 13.7 %copy-start.2 = (f32[1024,512]{1,0:T(8,128)}, f32[1024,512]{1,0:T(8,128)S(1)}, u32[]{:S(2)}) copy-start(f32[1024,512]{1,0:T(8,128)S(1)} %get-tuple-element.306) | copy-start | bytes 6291460
  297.1 4.8 copy-start.15
  297.1 4.8 copy-start.40
  306.9 3.4 copy-start.11
  311.5 1.4 copy-start.9
  335.6 73.8 %all-to-all-start.3 = ((bf16[4,768,512]{2,1,0:T(8,128)(2,1)}), bf16[4,768,512]{2,1,0:T(8,128)(2,1)S(1)}, u32[]{:S(2)}, u32[]{:S(2)}) async-start(bf16[4,768,512]{2,1,0:T(8,128)(2,1)} %bitcast.193), calls=%async_computation.3 | async-start | bytes 6291456 | tf_op jit(solution)/shard_map/all_to_all | solution.py:207
  339.3 166.7 %reduce-scatter.2.cloned.1.call-start = ((), (), s32[]{:S(2)}) async-start(), calls=%async_computation.7 | async-start | bytes 1310720 | tf_op jit(solution)/shard_map/reduce_scatter | solution.py:238
  479.6 209.7 %all-reduce.9.cloned.1.call-start = ((), (), s32[]{:S(2)}) async-start(), calls=%async_computation.8 | async-start | bytes 17301504 | tf_op jit(solution)/shard_map/psum | solution.py:264
  480.1 7.0 copy-start.3
  480.1 7.0 copy-start.12
  480.1 7.0 copy-start.35
  487.1 18.9 %copy-start.5 = (bf16[1024,512]{1,0:T(8,128)(2,1)S(1)}, bf16[1024,512]{1,0:T(8,128)(2,1)}, u32[]{:S(2)}) copy-start(bf16[1024,512]{1,0:T(8,128)(2,1)} %copy-done.4) | copy-start | bytes 3145732
  508.2 1.0 copy-start.16
  508.2 1.7 copy-start.17
  508.2 238.1 %all-reduce.13.cloned.1.call-start = ((), (), s32[]{:S(2)}) async-start(), calls=%async_computation.10 | async-start | bytes 262144 | tf_op jit(solution)/shard_map/psum | solution.py:247
  510.6 416.3 %all-reduce.11.cloned.1.call-start = ((), (), s32[]{:S(2)}) async-start(), calls=%async_computation.9 | async-start | bytes 17301504 | tf_op jit(solution)/shard_map/psum | solution.py:263
  689.4 74.6 %all-to-all-start.4 = ((bf16[4,768,512]{2,1,0:T(8,128)(2,1)}), bf16[4,768,512]{2,1,0:T(8,128)(2,1)S(1)}, u32[]{:S(2)}, u32[]{:S(2)}) async-start(bf16[4,768,512]{2,1,0:T(8,128)(2,1)} %get-tuple-element.155), calls=%async_computation.5 | async-start | bytes 6291456 | tf_op jit(solution)/shard_map/all_to_all | solution.py:237
  693.2 7.2 copy-start.30
  693.2 7.2 copy-start.21
  702.5 46.8 %copy-start.14 = (bf16[1024,128]{1,0:T(8,128)(2,1)S(1)}, bf16[1024,128]{1,0:T(8,128)(2,1)}, u32[]{:S(2)}) copy-start(bf16[1024,128]{1,0:T(8,128)(2,1)} %reduce-scatter.2.cloned.1.call-done) | copy-start | bytes 786436
  702.5 46.8 %copy-start.19 = (bf16[512,128]{1,0:T(8,128)(2,1)S(1)}, bf16[512,128]{1,0:T(8,128)(2,1)}, u32[]{:S(2)}) copy-start(bf16[512,128]{1,0:T(8,128)(2,1)} %param.21) | copy-start | bytes 393220
  702.5 61.5 %copy-start.25 = (s32[2048]{0:T(1024)S(1)}, s32[2048]{0:T(1024)}, u32[]{:S(2)}) copy-start(s32[2048]{0:T(1024)} %copy-done.24) | copy-start | bytes 24580
  778.8 8.6 copy-start.8
  778.8 8.6 copy-start.23
  778.8 8.6 copy-start.27
  778.8 8.6 copy-start.33
  778.8 8.6 copy-start.37
  787.4 4.8 copy-start.31
  787.4 4.7 copy-start.39
  787.4 48.1 %copy-start.10 = (f32[1024,512]{1,0:T(8,128)S(1)}, f32[1024,512]{1,0:T(8,128)}, u32[]{:S(2)}) copy-start(f32[1024,512]{1,0:T(8,128)} %copy-done.9) | copy-start | bytes 6291460
  928.5 4.9 copy-start.13
  928.5 6.9 copy-start.1
  (3 other events, 1.9 us)
Sparse Core Ops, SparseCore 0:
  64.3 43.4 all-gather.2
  479.8 26.2 reduce-scatter.1
  509.4 179.8 all-reduce.8
  693.1 53.1 all-reduce.12
  750.1 176.6 all-reduce.10
